TPU v7x, 32 devices: a whole 2x2x4 slice. The times are simulated.
32 devices in a mesh: mem: 4 (over y, core), sub: 8 (over z, x).
Axes of the slice: x: 2, y: 2, z: 4, core: 2. Of those that a mesh axis runs over, the one named last changes fastest.
Arguments:
- prior_sample_array: float32 [80, 8, 24, 512], P('mem', 'sub'), may hold values from -6 to 6
- courant_x: float32 [8, 512], P('sub'), may hold values from -0.3 to 0.3
- courant_y: float32 [8, 512], P('sub'), may hold values from -0.3 to 0.3
- diffusion: float32 [8, 512], P('sub'), may hold values from 0.02 to 0.09
- obs_cell: int32 [4, 128], replicated, may hold values from 0 to 4095
- obs_value: float32 [4, 128], replicated, may hold values from -6 to 6
- obs_error: float32 [4, 128], replicated, may hold values from 0.2 to 1
- obs_weight: float32 [4, 128, 24], replicated, may hold values from -1.25 to 1.25
- taper_radius: float32 [4, 128], replicated, may hold values from 64 to 256
Outputs:
- analysis: float32 [80, 8, 24, 512], P(None, 'sub', None, 'mem')
All inputs are finite; a program needn't handle non-finite values.
Results may differ from a plain program's by a relative error of at most 0.0003.
Values sent between devices are 32-bit elements; how exact they have to be, the bound alone decides.
No kernel may reach another device: no remote copies, remote signals or barrier semaphores. Data moves between devices by JAX's collectives and lax.ppermute only.
A program may use at most 64 MiB of HBM per device.

v0:
```python
import jax
import jax.numpy as jnp
from jax import lax
from jax.sharding import PartitionSpec as P

highest = lax.Precision.HIGHEST


def padded_2(shard, sides, width):
    for axis, dim in sides:
        size, length = (lax.axis_size(axis), shard.shape[dim])
        up = [(i, (i + 1) % size) for i in range(size - 1)]
        down = [(j, i) for i, j in up]
        last = lax.slice_in_dim(shard, length - width, length, axis=dim)
        first = lax.slice_in_dim(shard, 0, width, axis=dim)
        before = lax.ppermute(last, axis, up)
        after = lax.ppermute(first, axis, down)
        shard = jnp.concatenate([before, shard, after], axis=dim)
    return shard


def gaspari(delta_row, delta_col, cutoff_radius, width):
    cyclic_shifted = (delta_col + width // 2) % width - width // 2
    row_dist = delta_row.astype(jnp.float32)
    col_dist = cyclic_shifted.astype(jnp.float32)
    ratio = jnp.sqrt(row_dist * row_dist + col_dist * col_dist) / cutoff_radius
    inner = (((-0.25 * ratio + 0.5) * ratio + 0.625) * ratio - 5.0 / 3.0) * ratio * ratio + 1.0
    bounded = jnp.maximum(ratio, 1.0)
    outer = (
        ((((ratio / 12.0 - 0.5) * ratio + 0.625) * ratio + 5.0 / 3.0) * ratio - 5.0) * ratio
        + 4.0
        - 2.0 / (3.0 * bounded)
    )
    return jnp.where(ratio <= 1.0, inner, jnp.where(ratio < 2.0, outer, 0.0))


def carried_quantity(
    center,
    west_cells,
    east_cells,
    north_cells,
    southern_neighbours,
    flow_x,
    meridional_velocity,
    mixing,
):
    result = (
        center
        - jnp.maximum(flow_x, 0.0) * (center - west_cells)
        - jnp.minimum(flow_x, 0.0) * (east_cells - center)
    )
    result = (
        result
        - jnp.maximum(meridional_velocity, 0.0) * (center - southern_neighbours)
        - jnp.minimum(meridional_velocity, 0.0) * (north_cells - center)
    )
    return result + mixing * (
        east_cells + west_cells + north_cells + southern_neighbours - 4.0 * center
    )


def obs_factors(obs_prior, obs_value, obs_error):
    members = obs_prior.shape[1]
    average = jnp.mean(obs_prior, axis=1)
    anomaly = obs_prior - average[:, None]
    covariance = jnp.dot(anomaly, anomaly.T, precision=highest) / (members - 1) + jnp.diag(
        obs_error
    )
    factor = jnp.linalg.cholesky(covariance)
    innovation = (obs_value - average)[:, None]
    midpoint_values = lax.linalg.triangular_solve(factor, innovation, left_side=True, lower=True)
    solved = lax.linalg.triangular_solve(
        factor, midpoint_values, left_side=True, lower=True, transpose_a=True
    )
    shifted = factor + jnp.diag(jnp.sqrt(obs_error))
    reduced = lax.linalg.triangular_solve(shifted, anomaly, left_side=True, lower=True)
    squared = lax.linalg.triangular_solve(
        factor, reduced, left_side=True, lower=True, transpose_a=True
    )
    return (anomaly, solved - squared)


def local_prior(existing_grid_values, obs_rows, obs_cols, weights, row_start, col_start):
    rows_dev = existing_grid_values.shape[1]
    cols_dev = existing_grid_values.shape[3]
    local_rows = obs_rows - row_start
    local_cols = obs_cols - col_start
    owned = (
        (local_rows >= 0) & (local_rows < rows_dev) & (local_cols >= 0) & (local_cols < cols_dev)
    )
    picked = existing_grid_values[
        :, jnp.clip(local_rows, 0, rows_dev - 1), :, jnp.clip(local_cols, 0, cols_dev - 1)
    ]
    values = jnp.einsum("kmc,kc->km", picked, weights, precision=highest)
    return jnp.where(owned[:, None], values, 0.0)


def apply_update(existing_grid_values, obs_anomaly, coeffs, taper_cells, members):
    average = jnp.mean(existing_grid_values, axis=0)
    anomaly = existing_grid_values - average[None]
    cross_cov = jnp.einsum("mrcx,km->rcxk", anomaly, obs_anomaly, precision=highest) / (members - 1)
    gain = cross_cov * taper_cells[:, None, :, :]
    return existing_grid_values + jnp.einsum("rcxk,km->mrcx", gain, coeffs, precision=highest)


def shards(
    prior_sample_array,
    courant_x,
    courant_y,
    diffusion,
    obs_cell,
    obs_value,
    obs_error,
    obs_weight,
    taper_radius,
):
    width = courant_x.shape[1]
    rows_dev = prior_sample_array.shape[1]
    cols_dev = width // lax.axis_size("mem")
    members = prior_sample_array.shape[0] * lax.axis_size("mem")
    col_start = lax.axis_index("mem") * cols_dev
    row_start = lax.axis_index("sub") * rows_dev
    padded = padded_2(prior_sample_array, (("sub", 1),), 1)
    propagated_grids = carried_quantity(
        prior_sample_array,
        jnp.roll(prior_sample_array, 1, axis=3),
        jnp.roll(prior_sample_array, -1, axis=3),
        padded[:, 2:],
        padded[:, :-2],
        courant_x[:, None, :],
        courant_y[:, None, :],
        diffusion[:, None, :],
    )
    existing_grid_values = lax.all_to_all(
        propagated_grids, "mem", split_axis=3, concat_axis=0, tiled=True
    )
    row_ids = row_start + jnp.arange(rows_dev, dtype=jnp.int32)
    col_ids = col_start + jnp.arange(cols_dev, dtype=jnp.int32)
    obs_rows = obs_cell // width
    obs_cols = obs_cell % width
    batches = obs_cell.shape[0]

    def taper_cells(batch_index):
        return gaspari(
            row_ids[:, None, None] - obs_rows[batch_index][None, None, :],
            col_ids[None, :, None] - obs_cols[batch_index][None, None, :],
            taper_radius[batch_index][None, None, :],
            width,
        )

    for batch_index in range(batches):
        obs_prior = lax.psum(
            local_prior(
                existing_grid_values,
                obs_rows[batch_index],
                obs_cols[batch_index],
                obs_weight[batch_index],
                row_start,
                col_start,
            ),
            ("mem", "sub"),
        )
        obs_anomaly, coeffs = obs_factors(obs_prior, obs_value[batch_index], obs_error[batch_index])
        existing_grid_values = apply_update(
            existing_grid_values, obs_anomaly, coeffs, taper_cells(batch_index), members
        )
    return existing_grid_values


def solution(mesh):
    return jax.shard_map(
        shards,
        mesh=mesh,
        in_specs=(
            P("mem", "sub", None, None),
            P("sub", None),
            P("sub", None),
            P("sub", None),
            P(),
            P(),
            P(),
            P(),
            P(),
        ),
        out_specs=P(None, "sub", None, "mem"),
        check_vma=False,
    )
```

profile of v0, /device:TPU:0, one launch (start us, length us, event | category | flops | bytes accessed | tf_op | source)
XLA Modules:
  0.0 428.5 jit_solution(3687478982285887635)
XLA Ops:
  0.0 5.9 %collective-permute-start = (f32[20,1,24,512]{3,2,1,0:T(8,128)}, f32[20,1,24,512]{3,2,1,0:T(8,128)}, u32[]{:S(2)}, u32[]{:S(2)}) collective-permute-start(f32[20,1,24,512]{3,2,1,0:T(8,128)} %param.18), channel_id=1, source_target_pairs={{0,1},{1,2},{2,3},{3,4},{4,5},{5,6},{6,7},{8,9},{9,10},{10,11},{11... | collective-permute-start | bytes 2949128 | tf_op jit(solution)/shard_map/ppermute | solution.py:16
  14.5 32.9 %collective-permute-done = f32[20,1,24,512]{3,2,1,0:T(8,128)} collective-permute-done((f32[20,1,24,512]{3,2,1,0:T(8,128)}, f32[20,1,24,512]{3,2,1,0:T(8,128)}, u32[]{:S(2)}, u32[]{:S(2)}) %collective-permute-start) | collective-permute-done | bytes 983072 | tf_op jit(solution)/shard_map/ppermute | solution.py:16
  50.7 4.3 copy.87
  54.9 6.5 %reshape.1524 = f32[4,1,61440]{2,1,0:T(1,128)} reshape(f32[512,1,20,24]{3,2,1,0:T(8,128)} %bitcast.330) | data formatting | bytes 1966080
  61.5 4.1 all-to-all-start
  68.4 10.9 %all-to-all-done = f32[4,1,61440]{2,1,0:T(1,128)S(1)} async-done(((f32[4,1,61440]{2,1,0:T(1,128)}), f32[4,1,61440]{2,1,0:T(1,128)S(1)}, u32[]{:S(2)}, u32[]{:S(2)}) %all-to-all-start) | async-done | bytes 983072 | tf_op jit(solution)/shard_map/all_to_all | solution.py:134
  83.3 6.0 %reshape.1525 = f32[512,1,20,24]{3,2,1,0:T(8,128)} reshape(f32[4,61440]{1,0:T(4,128)S(1)} %reduce.20) | data formatting | bytes 1966080
  89.4 5.6 %copy.88 = f32[20,1,24,512]{3,1,2,0:T(1,128)S(1)} copy(f32[20,1,24,512]{2,0,1,3:T(8,128)} %bitcast.331) | data formatting | bytes 1966080 | tf_op jit(solution)/shard_map/all_to_all | solution.py:134
  99.2 41.8 %psum.28 = f32[128,80]{0,1:T(8,128)S(1)} all-reduce(f32[128,80]{0,1:T(8,128)S(1)} %broadcast_select_fusion.3), channel_id=1, replica_groups=mesh['mem'=4,'sub'=8] {'mem','sub'}, use_global_device_ids=true, to_apply=%region_0.1 | all-reduce | flops 10240 | bytes 81920 | tf_op jit(solution)/shard_map/psum | solution.py:152
  143.0 11.7 %cholesky.74 = f32[128,128]{1,0:T(8,128)S(1)} custom-call(f32[128,128]{1,0:T(8,128)S(1)} %copy.93), custom_call_target="Cholesky" | custom-call | tf_op jit(solution)/shard_map/jit(cholesky)/cholesky | solution.py:69
  156.1 9.8 %custom-call.36 = f32[1,128,128]{1,2,0:T(8,128)S(1)} custom-call(f32[1,128,128]{2,1,0:T(8,128)S(1)} %get-tuple-element.21), custom_call_target="InvertDiagBlocksLowerTriangular" | custom-call | tf_op jit(solution)/shard_map/triangular_solve/custom-call.3 | solution.py:76
  166.1 9.8 %custom-call.35 = f32[1,128,128]{1,2,0:T(8,128)S(1)} custom-call(f32[1,128,128]{2,1,0:T(8,128)S(1)} %get-tuple-element.20), custom_call_target="InvertDiagBlocksLowerTriangular" | custom-call | tf_op jit(solution)/shard_map/triangular_solve/custom-call.2 | solution.py:72
  184.5 40.4 %psum.29 = f32[128,80]{0,1:T(8,128)S(1)} all-reduce(f32[128,80]{0,1:T(8,128)S(1)} %broadcast_select_fusion.2), channel_id=1, replica_groups=mesh['mem'=4,'sub'=8] {'mem','sub'}, use_global_device_ids=true, to_apply=%region_5.11 | all-reduce | flops 10240 | bytes 81920 | tf_op jit(solution)/shard_map/psum | solution.py:152
  225.5 11.7 %cholesky.85 = f32[128,128]{1,0:T(8,128)S(1)} custom-call(f32[128,128]{1,0:T(8,128)S(1)} %copy.98), custom_call_target="Cholesky" | custom-call | tf_op jit(solution)/shard_map/jit(cholesky)/cholesky | solution.py:69
  238.7 9.8 %custom-call.40 = f32[1,128,128]{1,2,0:T(8,128)S(1)} custom-call(f32[1,128,128]{2,1,0:T(8,128)S(1)} %get-tuple-element.19), custom_call_target="InvertDiagBlocksLowerTriangular" | custom-call | tf_op jit(solution)/shard_map/triangular_solve/custom-call.3 | solution.py:76
  248.7 9.8 %custom-call.39 = f32[1,128,128]{1,2,0:T(8,128)S(1)} custom-call(f32[1,128,128]{2,1,0:T(8,128)S(1)} %get-tuple-element.18), custom_call_target="InvertDiagBlocksLowerTriangular" | custom-call | tf_op jit(solution)/shard_map/triangular_solve/custom-call.2 | solution.py:72
  266.2 40.3 %psum.30 = f32[128,80]{0,1:T(8,128)S(1)} all-reduce(f32[128,80]{0,1:T(8,128)S(1)} %broadcast_select_fusion.1), channel_id=1, replica_groups=mesh['mem'=4,'sub'=8] {'mem','sub'}, use_global_device_ids=true, to_apply=%region_8.14 | all-reduce | flops 10240 | bytes 81920 | tf_op jit(solution)/shard_map/psum | solution.py:152
  307.1 11.7 %cholesky.96 = f32[128,128]{1,0:T(8,128)S(1)} custom-call(f32[128,128]{1,0:T(8,128)S(1)} %copy.101), custom_call_target="Cholesky" | custom-call | tf_op jit(solution)/shard_map/jit(cholesky)/cholesky | solution.py:69
  320.2 9.8 %custom-call.44 = f32[1,128,128]{1,2,0:T(8,128)S(1)} custom-call(f32[1,128,128]{2,1,0:T(8,128)S(1)} %get-tuple-element.17), custom_call_target="InvertDiagBlocksLowerTriangular" | custom-call | tf_op jit(solution)/shard_map/triangular_solve/custom-call.3 | solution.py:76
  330.2 9.8 %custom-call.43 = f32[1,128,128]{1,2,0:T(8,128)S(1)} custom-call(f32[1,128,128]{2,1,0:T(8,128)S(1)} %get-tuple-element.16), custom_call_target="InvertDiagBlocksLowerTriangular" | custom-call | tf_op jit(solution)/shard_map/triangular_solve/custom-call.2 | solution.py:72
  347.7 40.6 %psum.31 = f32[128,80]{0,1:T(8,128)S(1)} all-reduce(f32[128,80]{0,1:T(8,128)S(1)} %broadcast_select_fusion), channel_id=1, replica_groups=mesh['mem'=4,'sub'=8] {'mem','sub'}, use_global_device_ids=true, to_apply=%region_11.17 | all-reduce | flops 10240 | bytes 81920 | tf_op jit(solution)/shard_map/psum | solution.py:152
  388.9 11.7 %cholesky.107 = f32[128,128]{1,0:T(8,128)S(1)} custom-call(f32[128,128]{1,0:T(8,128)S(1)} %copy.104), custom_call_target="Cholesky" | custom-call | tf_op jit(solution)/shard_map/jit(cholesky)/cholesky | solution.py:69
  402.2 9.8 %custom-call.48 = f32[1,128,128]{1,2,0:T(8,128)S(1)} custom-call(f32[1,128,128]{2,1,0:T(8,128)S(1)} %get-tuple-element.15), custom_call_target="InvertDiagBlocksLowerTriangular" | custom-call | tf_op jit(solution)/shard_map/triangular_solve/custom-call.3 | solution.py:76
  412.2 9.8 %custom-call.47 = f32[1,128,128]{1,2,0:T(8,128)S(1)} custom-call(f32[1,128,128]{2,1,0:T(8,128)S(1)} %get-tuple-element.14), custom_call_target="InvertDiagBlocksLowerTriangular" | custom-call | tf_op jit(solution)/shard_map/triangular_solve/custom-call.2 | solution.py:72
  (169 shorter events, 62.6 us)
Async XLA Ops:
  0.0 14.1 %copy-start.8 = (f32[20,1,24,512]{3,2,1,0:T(8,128)S(1)}, f32[20,1,24,512]{3,2,1,0:T(8,128)}, u32[]{:S(2)}) copy-start(f32[20,1,24,512]{3,2,1,0:T(8,128)} %param.18) | copy-start | bytes 2949124
  0.0 47.4 %collective-permute-start = (f32[20,1,24,512]{3,2,1,0:T(8,128)}, f32[20,1,24,512]{3,2,1,0:T(8,128)}, u32[]{:S(2)}, u32[]{:S(2)}) collective-permute-start(f32[20,1,24,512]{3,2,1,0:T(8,128)} %param.18), channel_id=1, source_target_pairs={{0,1},{1,2},{2,3},{3,4},{4,5},{5,6},{6,7},{8,9},{9,10},{10,11},{11... | collective-permute-start | bytes 2949128 | tf_op jit(solution)/shard_map/ppermute | solution.py:16
  5.9 41.4 %collective-permute-start.1 = (f32[20,1,24,512]{3,2,1,0:T(8,128)}, f32[20,1,24,512]{3,2,1,0:T(8,128)S(1)}, u32[]{:S(2)}, u32[]{:S(2)}) collective-permute-start(f32[20,1,24,512]{3,2,1,0:T(8,128)} %param.18), channel_id=1, source_target_pairs={{1,0},{2,1},{3,2},{4,3},{5,4},{6,5},{7,6},{9,8},{10,9},{11,10},{12... | collective-permute-start | bytes 2949128 | tf_op jit(solution)/shard_map/ppermute | solution.py:17
  14.1 34.2 %copy-start.15 = (f32[1,512]{1,0:T(1,128)S(1)}, f32[1,512]{1,0:T(1,128)}, u32[]{:S(2)}) copy-start(f32[1,512]{1,0:T(1,128)} %param.21) | copy-start | bytes 6148
  61.5 6.4 %copy-start.28 = (f32[4,128]{1,0:T(4,128)S(1)}, f32[4,128]{1,0:T(4,128)}, u32[]{:S(2)}) copy-start(f32[4,128]{1,0:T(4,128)} %param.26) | copy-start | bytes 6148
  61.5 17.8 %all-to-all-start = ((f32[4,1,61440]{2,1,0:T(1,128)}), f32[4,1,61440]{2,1,0:T(1,128)S(1)}, u32[]{:S(2)}, u32[]{:S(2)}) async-start(f32[4,1,61440]{2,1,0:T(1,128)} %reshape.1524), calls=%async_computation | async-start | bytes 1966080 | tf_op jit(solution)/shard_map/all_to_all | solution.py:134
  94.9 0.9 copy-start.9
  95.9 1.0 copy-start.6
  97.7 1.5 copy-start.19
  97.7 44.8 %copy-start.27 = (f32[128]{0:T(128)S(1)}, f32[128]{0:T(128)}, u32[]{:S(2)}) copy-start(f32[128]{0:T(128)} %get-tuple-element.52) | copy-start | bytes 1540
  97.7 57.7 %copy-start.26 = (f32[128]{0:T(128)S(1)}, f32[128]{0:T(128)}, u32[]{:S(2)}) copy-start(f32[128]{0:T(128)} %get-tuple-element.49) | copy-start | bytes 1540
  99.1 76.8 %copy-start.13 = (f32[4,128]{1,0:T(4,128)S(1)}, f32[4,128]{1,0:T(4,128)}, u32[]{:S(2)}) copy-start(f32[4,128]{1,0:T(4,128)} %param.23) | copy-start | bytes 6148
  99.1 77.2 %copy-start.7 = (f32[4,20,1,24,128]{4,3,1,0,2:T(8,128)S(1)}, f32[4,20,1,24,128]{4,3,1,0,2:T(8,128)}, u32[]{:S(2)}) copy-start(f32[4,20,1,24,128]{4,3,1,0,2:T(8,128)} %copy-done.6) | copy-start | bytes 2949124
  183.9 41.1 %copy-start.25 = (f32[128]{0:T(128)S(1)}, f32[128]{0:T(128)}, u32[]{:S(2)}) copy-start(f32[128]{0:T(128)} %get-tuple-element.51) | copy-start | bytes 1540
  183.9 54.1 %copy-start.24 = (f32[128]{0:T(128)S(1)}, f32[128]{0:T(128)}, u32[]{:S(2)}) copy-start(f32[128]{0:T(128)} %get-tuple-element.48) | copy-start | bytes 1540
  183.9 75.0 %copy-start.12 = (f32[24,128]{1,0:T(8,128)S(1)}, f32[24,128]{1,0:T(8,128)}, u32[]{:S(2)}) copy-start(f32[24,128]{1,0:T(8,128)} %get-tuple-element.64) | copy-start | bytes 36868
  183.9 75.0 %copy-start.3 = (f32[80,24,128]{2,0,1:T(8,128)S(1)}, f32[80,24,128]{2,0,1:T(8,128)}, u32[]{:S(2)}) copy-start(f32[80,24,128]{2,0,1:T(8,128)} %copy-done.2) | copy-start | bytes 2949124
  265.5 41.0 %copy-start.23 = (f32[128]{0:T(128)S(1)}, f32[128]{0:T(128)}, u32[]{:S(2)}) copy-start(f32[128]{0:T(128)} %get-tuple-element.53) | copy-start | bytes 1540
  265.5 54.0 %copy-start.22 = (f32[128]{0:T(128)S(1)}, f32[128]{0:T(128)}, u32[]{:S(2)}) copy-start(f32[128]{0:T(128)} %get-tuple-element.47) | copy-start | bytes 1540
  265.5 74.9 %copy-start.5 = (f32[80,24,128]{2,0,1:T(8,128)S(1)}, f32[80,24,128]{2,0,1:T(8,128)}, u32[]{:S(2)}) copy-start(f32[80,24,128]{2,0,1:T(8,128)} %copy-done.4) | copy-start | bytes 2949124
  347.1 41.3 %copy-start.21 = (f32[128]{0:T(128)S(1)}, f32[128]{0:T(128)}, u32[]{:S(2)}) copy-start(f32[128]{0:T(128)} %get-tuple-element.50) | copy-start | bytes 1540
  347.1 54.3 %copy-start.20 = (f32[128]{0:T(128)S(1)}, f32[128]{0:T(128)}, u32[]{:S(2)}) copy-start(f32[128]{0:T(128)} %get-tuple-element.46) | copy-start | bytes 1540
  347.1 74.9 %copy-start.14 = (f32[4,128]{1,0:T(4,128)S(1)}, f32[4,128]{1,0:T(4,128)}, u32[]{:S(2)}) copy-start(f32[4,128]{1,0:T(4,128)} %param.23) | copy-start | bytes 6148
  347.1 75.3 %copy-start.1 = (f32[80,24,128]{2,0,1:T(8,128)S(1)}, f32[80,24,128]{2,0,1:T(8,128)}, u32[]{:S(2)}) copy-start(f32[80,24,128]{2,0,1:T(8,128)} %copy-done) | copy-start | bytes 2949124
  (8 other events, 6.6 us)
where the time goes:
time: 432 us; the launch traced here: 428 us
  blocking collectives  163 us (38%)
  other arithmetic  145 us (34%)
  waiting for transfers between devices  43.8 us (10%)
  local copies, waits for them, and re-layouts  41.1 us (10%)
  matrix products  23.1 us (5%)
  starting transfers between devices  11.3 us (3%)
    psum x4, blocking collectives, shards(): lax.psum(local_prior(existing_grid_values, obs_rows[batch_index], obs_col...  163 us
    another operation x12, other arithmetic, obs_factors(): factor = jnp.linalg.cholesky(covariance)  49.7 us
    another operation x8, other arithmetic, obs_factors(): lax.linalg.triangular_solve(factor, midpoint_values, left_side=True, lowe...  42.2 us
    another operation x4, other arithmetic, obs_factors(): lax.linalg.triangular_solve(shifted, anomaly, left_side=True, lower=True)  39.2 us
    ppermute x1, waiting for transfers between devices, padded_2(): before = lax.ppermute(last, axis, up)  32.9 us
    unnamed x64, local copies, waits for them, and re-layouts  17.7 us
    all_to_all x1, waiting for transfers between devices, shards(): lax.all_to_all(propagated_grids, 'mem', split_axis=3, concat_axis=0, tile...  10.9 us
    dot_general x4, matrix products, apply_update(): jnp.einsum('mrcx,km->rcxk', anomaly, obs_anomaly, precision=highest)  10.5 us
  transfers between devices with their start and end apart: 3, of which 2 were waited for; matrix products, arithmetic and copies ran while one was open for 2% of the time, Pallas kernels for 0%

commit v1 on v0

--- a/solution.py
+++ b/solution.py
@@ -4,6 +4,22 @@
 from jax.sharding import PartitionSpec as P
 
 highest = lax.Precision.HIGHEST
+
+
+def _manage_squares(panel, where_dim, own_rows):
+    answer = panel.shape
+    everything = panel.reshape(
+        *answer[:where_dim], own_rows, answer[where_dim] // own_rows, *answer[where_dim + 1 :]
+    )
+    response = jnp.moveaxis(everything, where_dim, 0)
+    return response
+
+
+def bind_stacks_all_on_mesh(here_x, d_out):
+    clean = list(here_x.shape[1:])
+    clean[d_out] *= here_x.shape[0]
+    v_now = jnp.moveaxis(here_x, 0, d_out).reshape(clean)
+    return v_now
 
 
 def padded_2(shard, sides, width):
@@ -131,9 +147,20 @@
         courant_y[:, None, :],
         diffusion[:, None, :],
     )
-    existing_grid_values = lax.all_to_all(
-        propagated_grids, "mem", split_axis=3, concat_axis=0, tiled=True
-    )
+    t1 = lax.axis_size("mem")
+    out_arr = lax.axis_index("mem")
+    work_now, local_next = (t1, out_arr)
+    n_now = _manage_squares(propagated_grids, 3, work_now)
+    row_list = [n_now[local_next]]
+    for hop_no in [*range(1, work_now)]:
+        plain = n_now[(local_next + hop_no) % work_now]
+        long_array = lax.ppermute(
+            plain, "mem", [(jj, (jj + hop_no) % work_now) for jj in range(work_now)]
+        )
+        row_list.append(long_array)
+    next_value = jnp.stack(row_list, axis=0)
+    n_now = next_value[(local_next - jnp.arange(work_now)) % work_now]
+    existing_grid_values = bind_stacks_all_on_mesh(n_now, 0)
     row_ids = row_start + jnp.arange(rows_dev, dtype=jnp.int32)
     col_ids = col_start + jnp.arange(cols_dev, dtype=jnp.int32)
     obs_rows = obs_cell // width

time: 432 us -> 404 us (0.935)
  local copies, waits for them, and re-layouts: 41.1 us -> 18.2 us
    unnamed x64 -> x56, local copies, waits for them, and re-layouts: 17.7 us -> 3.26 us
    all_to_all x1 -> x0, waiting for transfers between devices: 10.9 us -> none  [shards(): lax.all_to_all(propagated_grids, 'mem', split_axis=3, concat_axis=0, tile...]
    ppermute x0 -> x3, waiting for transfers between devices: none -> 9.65 us  [shards(): lax.ppermute(plain, 'mem', [(jj, (jj + hop_no) % work_now) for jj in rang...]
    all_to_all x4 -> x0, local copies, waits for them, and re-layouts: 6.76 us -> none  [shards(): lax.all_to_all(propagated_grids, 'mem', split_axis=3, concat_axis=0, tile...]
  transfers between devices with their start and end apart: 3 -> 5, of which waited for: 2 -> 4; matrix products, arithmetic and copies ran while one was open for 2% -> 3% of each run, Pallas kernels for 0% -> 0%
where the time goes in v1:
time: 404 us; the launch traced here: 398 us
  blocking collectives  164 us (41%)
  other arithmetic  141 us (35%)
  waiting for transfers between devices  41 us (10%)
  matrix products  23.2 us (6%)
  local copies, waits for them, and re-layouts  18.2 us (5%)
  starting transfers between devices  9.02 us (2%)
    psum x4, blocking collectives, shards(): lax.psum(local_prior(existing_grid_values, obs_rows[batch_index], obs_col...  164 us
    another operation x12, other arithmetic, obs_factors(): factor = jnp.linalg.cholesky(covariance)  49.7 us
    another operation x8, other arithmetic, obs_factors(): lax.linalg.triangular_solve(factor, midpoint_values, left_side=True, lowe...  42.1 us
    another operation x4, other arithmetic, obs_factors(): lax.linalg.triangular_solve(shifted, anomaly, left_side=True, lower=True)  39.2 us
    ppermute x1, waiting for transfers between devices, padded_2(): before = lax.ppermute(last, axis, up)  31.4 us
    dot_general x4, matrix products, apply_update(): jnp.einsum('mrcx,km->rcxk', anomaly, obs_anomaly, precision=highest)  10.5 us
    ppermute x3, waiting for transfers between devices, shards(): lax.ppermute(plain, 'mem', [(jj, (jj + hop_no) % work_now) for jj in rang...  9.65 us
    dot_general x4, matrix products, apply_update(): jnp.einsum('rcxk,km->mrcx', gain, coeffs, precision=highest)  8.39 us
  transfers between devices with their start and end apart: 5, of which 4 were waited for; matrix products, arithmetic and copies ran while one was open for 3% of the time, Pallas kernels for 0%

profile of v1, /device:TPU:0, one launch (start us, length us, event | category | flops | bytes accessed | tf_op | source)
XLA Modules:
  0.0 397.9 jit_solution(12732306436222194960)
XLA Ops:
  0.0 5.9 %collective-permute-start = (f32[20,1,24,512]{3,2,1,0:T(8,128)}, f32[20,1,24,512]{3,2,1,0:T(8,128)}, u32[]{:S(2)}, u32[]{:S(2)}) collective-permute-start(f32[20,1,24,512]{3,2,1,0:T(8,128)} %param.18), channel_id=1, source_target_pairs={{0,1},{1,2},{2,3},{3,4},{4,5},{5,6},{6,7},{8,9},{9,10},{10,11},{11... | collective-permute-start | bytes 2949128 | tf_op jit(solution)/shard_map/ppermute | solution.py:32
  16.0 31.4 %collective-permute-done = f32[20,1,24,512]{3,2,1,0:T(8,128)} collective-permute-done((f32[20,1,24,512]{3,2,1,0:T(8,128)}, f32[20,1,24,512]{3,2,1,0:T(8,128)}, u32[]{:S(2)}, u32[]{:S(2)}) %collective-permute-start) | collective-permute-done | bytes 983072 | tf_op jit(solution)/shard_map/ppermute | solution.py:32
  56.6 8.1 %collective-permute-done.3 = f32[20,1,24,128]{3,2,0,1:T(8,128)S(1)} collective-permute-done((f32[20,1,24,128]{3,2,0,1:T(8,128)S(1)}, f32[20,1,24,128]{3,2,0,1:T(8,128)S(1)}, u32[]{:S(2)}, u32[]{:S(2)}) %collective-permute-start.3) | collective-permute-done | bytes 245792 | tf_op jit(solution)/shard_map/ppermute | solution.py:157
  68.8 42.1 %psum.28 = f32[128,80]{0,1:T(8,128)S(1)} all-reduce(f32[128,80]{0,1:T(8,128)S(1)} %broadcast_select_fusion.3), channel_id=1, replica_groups=mesh['mem'=4,'sub'=8] {'mem','sub'}, use_global_device_ids=true, to_apply=%region_0.1 | all-reduce | flops 10240 | bytes 81920 | tf_op jit(solution)/shard_map/psum | solution.py:179
  111.5 11.7 %cholesky.74 = f32[128,128]{1,0:T(8,128)S(1)} custom-call(f32[128,128]{1,0:T(8,128)S(1)} %copy.43), custom_call_target="Cholesky" | custom-call | tf_op jit(solution)/shard_map/jit(cholesky)/cholesky | solution.py:85
  124.7 9.8 %custom-call.36 = f32[1,128,128]{1,2,0:T(8,128)S(1)} custom-call(f32[1,128,128]{2,1,0:T(8,128)S(1)} %get-tuple-element.25), custom_call_target="InvertDiagBlocksLowerTriangular" | custom-call | tf_op jit(solution)/shard_map/triangular_solve/custom-call.3 | solution.py:92
  134.7 9.8 %custom-call.35 = f32[1,128,128]{1,2,0:T(8,128)S(1)} custom-call(f32[1,128,128]{2,1,0:T(8,128)S(1)} %get-tuple-element.24), custom_call_target="InvertDiagBlocksLowerTriangular" | custom-call | tf_op jit(solution)/shard_map/triangular_solve/custom-call.2 | solution.py:88
  145.0 2.6 fusion.31
  147.9 2.8 fusion.188
  153.2 41.4 %psum.29 = f32[128,80]{0,1:T(8,128)S(1)} all-reduce(f32[128,80]{0,1:T(8,128)S(1)} %broadcast_select_fusion.2), channel_id=1, replica_groups=mesh['mem'=4,'sub'=8] {'mem','sub'}, use_global_device_ids=true, to_apply=%region_5.11 | all-reduce | flops 10240 | bytes 81920 | tf_op jit(solution)/shard_map/psum | solution.py:179
  195.1 11.7 %cholesky.85 = f32[128,128]{1,0:T(8,128)S(1)} custom-call(f32[128,128]{1,0:T(8,128)S(1)} %copy.48), custom_call_target="Cholesky" | custom-call | tf_op jit(solution)/shard_map/jit(cholesky)/cholesky | solution.py:85
  208.1 9.8 %custom-call.40 = f32[1,128,128]{1,2,0:T(8,128)S(1)} custom-call(f32[1,128,128]{2,1,0:T(8,128)S(1)} %get-tuple-element.23), custom_call_target="InvertDiagBlocksLowerTriangular" | custom-call | tf_op jit(solution)/shard_map/triangular_solve/custom-call.3 | solution.py:92
  218.1 9.8 %custom-call.39 = f32[1,128,128]{1,2,0:T(8,128)S(1)} custom-call(f32[1,128,128]{2,1,0:T(8,128)S(1)} %get-tuple-element.22), custom_call_target="InvertDiagBlocksLowerTriangular" | custom-call | tf_op jit(solution)/shard_map/triangular_solve/custom-call.2 | solution.py:88
  228.3 2.6 fusion.37
  235.6 39.5 %psum.30 = f32[128,80]{0,1:T(8,128)S(1)} all-reduce(f32[128,80]{0,1:T(8,128)S(1)} %broadcast_select_fusion.1), channel_id=1, replica_groups=mesh['mem'=4,'sub'=8] {'mem','sub'}, use_global_device_ids=true, to_apply=%region_8.14 | all-reduce | flops 10240 | bytes 81920 | tf_op jit(solution)/shard_map/psum | solution.py:179
  275.6 11.7 %cholesky.96 = f32[128,128]{1,0:T(8,128)S(1)} custom-call(f32[128,128]{1,0:T(8,128)S(1)} %copy.51), custom_call_target="Cholesky" | custom-call | tf_op jit(solution)/shard_map/jit(cholesky)/cholesky | solution.py:85
  288.7 9.8 %custom-call.44 = f32[1,128,128]{1,2,0:T(8,128)S(1)} custom-call(f32[1,128,128]{2,1,0:T(8,128)S(1)} %get-tuple-element.21), custom_call_target="InvertDiagBlocksLowerTriangular" | custom-call | tf_op jit(solution)/shard_map/triangular_solve/custom-call.3 | solution.py:92
  298.7 9.8 %custom-call.43 = f32[1,128,128]{1,2,0:T(8,128)S(1)} custom-call(f32[1,128,128]{2,1,0:T(8,128)S(1)} %get-tuple-element.20), custom_call_target="InvertDiagBlocksLowerTriangular" | custom-call | tf_op jit(solution)/shard_map/triangular_solve/custom-call.2 | solution.py:88
  309.0 2.6 fusion.35
  316.3 41.4 %psum.31 = f32[128,80]{0,1:T(8,128)S(1)} all-reduce(f32[128,80]{0,1:T(8,128)S(1)} %broadcast_select_fusion), channel_id=1, replica_groups=mesh['mem'=4,'sub'=8] {'mem','sub'}, use_global_device_ids=true, to_apply=%region_11.17 | all-reduce | flops 10240 | bytes 81920 | tf_op jit(solution)/shard_map/psum | solution.py:179
  358.2 11.7 %cholesky.107 = f32[128,128]{1,0:T(8,128)S(1)} custom-call(f32[128,128]{1,0:T(8,128)S(1)} %copy.54), custom_call_target="Cholesky" | custom-call | tf_op jit(solution)/shard_map/jit(cholesky)/cholesky | solution.py:85
  371.4 9.8 %custom-call.48 = f32[1,128,128]{1,2,0:T(8,128)S(1)} custom-call(f32[1,128,128]{2,1,0:T(8,128)S(1)} %get-tuple-element.19), custom_call_target="InvertDiagBlocksLowerTriangular" | custom-call | tf_op jit(solution)/shard_map/triangular_solve/custom-call.3 | solution.py:92
  381.4 9.8 %custom-call.47 = f32[1,128,128]{1,2,0:T(8,128)S(1)} custom-call(f32[1,128,128]{2,1,0:T(8,128)S(1)} %get-tuple-element.18), custom_call_target="InvertDiagBlocksLowerTriangular" | custom-call | tf_op jit(solution)/shard_map/triangular_solve/custom-call.2 | solution.py:88
  391.7 2.6 fusion.33
  (166 shorter events, 48.2 us)
Async XLA Ops:
  0.0 15.6 %copy-start.8 = (f32[20,1,24,512]{3,2,1,0:T(8,128)S(1)}, f32[20,1,24,512]{3,2,1,0:T(8,128)}, u32[]{:S(2)}) copy-start(f32[20,1,24,512]{3,2,1,0:T(8,128)} %param.18) | copy-start | bytes 2949124
  0.0 47.4 %collective-permute-start = (f32[20,1,24,512]{3,2,1,0:T(8,128)}, f32[20,1,24,512]{3,2,1,0:T(8,128)}, u32[]{:S(2)}, u32[]{:S(2)}) collective-permute-start(f32[20,1,24,512]{3,2,1,0:T(8,128)} %param.18), channel_id=1, source_target_pairs={{0,1},{1,2},{2,3},{3,4},{4,5},{5,6},{6,7},{8,9},{9,10},{10,11},{11... | collective-permute-start | bytes 2949128 | tf_op jit(solution)/shard_map/ppermute | solution.py:32
  5.9 41.4 %collective-permute-start.1 = (f32[20,1,24,512]{3,2,1,0:T(8,128)}, f32[20,1,24,512]{3,2,1,0:T(8,128)}, u32[]{:S(2)}, u32[]{:S(2)}) collective-permute-start(f32[20,1,24,512]{3,2,1,0:T(8,128)} %param.18), channel_id=1, source_target_pairs={{1,0},{2,1},{3,2},{4,3},{5,4},{6,5},{7,6},{9,8},{10,9},{11,10},{12... | collective-permute-start | bytes 2949128 | tf_op jit(solution)/shard_map/ppermute | solution.py:33
  15.6 31.7 %copy-start.13 = (f32[1,512]{1,0:T(1,128)S(1)}, f32[1,512]{1,0:T(1,128)}, u32[]{:S(2)}) copy-start(f32[1,512]{1,0:T(1,128)} %param.21) | copy-start | bytes 6148
  51.1 5.5 %collective-permute-start.4 = (f32[20,1,24,128]{3,2,0,1:T(8,128)S(1)}, f32[20,1,24,128]{3,2,0,1:T(8,128)S(1)}, u32[]{:S(2)}, u32[]{:S(2)}) collective-permute-start(f32[20,1,24,128]{3,2,0,1:T(8,128)S(1)} %bitcast.355), channel_id=1, source_target_pairs={{0,24},{8,0},{16,8},{24,16},{1,25},{9,1},{17,9},{25,17},{2,26},{10... | collective-permute-start | bytes 737288 | tf_op jit(solution)/shard_map/ppermute | solution.py:157
  51.2 13.4 %collective-permute-start.3 = (f32[20,1,24,128]{3,2,0,1:T(8,128)S(1)}, f32[20,1,24,128]{3,2,0,1:T(8,128)S(1)}, u32[]{:S(2)}, u32[]{:S(2)}) collective-permute-start(f32[20,1,24,128]{3,2,0,1:T(8,128)S(1)} %bitcast.353), channel_id=1, source_target_pairs={{0,16},{8,24},{16,0},{24,8},{1,17},{9,25},{17,1},{25,9},{2,18},{10... | collective-permute-start | bytes 737288 | tf_op jit(solution)/shard_map/ppermute | solution.py:157
  52.7 12.0 %collective-permute-start.2 = (f32[20,1,24,128]{3,2,0,1:T(8,128)S(1)}, f32[20,1,24,128]{3,2,0,1:T(8,128)S(1)}, u32[]{:S(2)}, u32[]{:S(2)}) collective-permute-start(f32[20,1,24,128]{3,2,0,1:T(8,128)S(1)} %bitcast.352), channel_id=1, source_target_pairs={{0,8},{8,16},{16,24},{24,0},{1,9},{9,17},{17,25},{25,1},{2,10},{10... | collective-permute-start | bytes 737288 | tf_op jit(solution)/shard_map/ppermute | solution.py:157
  65.4 0.9 copy-start
  67.2 1.6 copy-start.17
  67.2 43.7 %copy-start.1 = (f32[4,20,24,128]{3,2,1,0:T(8,128)S(1)}, f32[4,20,24,128]{3,2,1,0:T(8,128)}, u32[]{:S(2)}) copy-start(f32[4,20,24,128]{3,2,1,0:T(8,128)} %copy-done) | copy-start | bytes 2949124
  67.2 43.8 %copy-start.25 = (f32[128]{0:T(128)S(1)}, f32[128]{0:T(128)}, u32[]{:S(2)}) copy-start(f32[128]{0:T(128)} %get-tuple-element.56) | copy-start | bytes 1540
  67.2 56.7 %copy-start.24 = (f32[128]{0:T(128)S(1)}, f32[128]{0:T(128)}, u32[]{:S(2)}) copy-start(f32[128]{0:T(128)} %get-tuple-element.53) | copy-start | bytes 1540
  68.7 75.8 %copy-start.11 = (f32[4,128]{1,0:T(4,128)S(1)}, f32[4,128]{1,0:T(4,128)}, u32[]{:S(2)}) copy-start(f32[4,128]{1,0:T(4,128)} %param.23) | copy-start | bytes 6148
  152.5 42.1 %copy-start.23 = (f32[128]{0:T(128)S(1)}, f32[128]{0:T(128)}, u32[]{:S(2)}) copy-start(f32[128]{0:T(128)} %get-tuple-element.55) | copy-start | bytes 1540
  152.5 55.0 %copy-start.22 = (f32[128]{0:T(128)S(1)}, f32[128]{0:T(128)}, u32[]{:S(2)}) copy-start(f32[128]{0:T(128)} %get-tuple-element.52) | copy-start | bytes 1540
  152.5 75.8 %copy-start.10 = (f32[24,128]{1,0:T(8,128)S(1)}, f32[24,128]{1,0:T(8,128)}, u32[]{:S(2)}) copy-start(f32[24,128]{1,0:T(8,128)} %get-tuple-element.68) | copy-start | bytes 36868
  152.5 75.8 %copy-start.5 = (f32[80,24,128]{2,0,1:T(8,128)S(1)}, f32[80,24,128]{2,0,1:T(8,128)}, u32[]{:S(2)}) copy-start(f32[80,24,128]{2,0,1:T(8,128)} %copy-done.4) | copy-start | bytes 2949124
  234.9 40.2 %copy-start.21 = (f32[128]{0:T(128)S(1)}, f32[128]{0:T(128)}, u32[]{:S(2)}) copy-start(f32[128]{0:T(128)} %get-tuple-element.57) | copy-start | bytes 1540
  234.9 53.1 %copy-start.20 = (f32[128]{0:T(128)S(1)}, f32[128]{0:T(128)}, u32[]{:S(2)}) copy-start(f32[128]{0:T(128)} %get-tuple-element.51) | copy-start | bytes 1540
  234.9 74.0 %copy-start.7 = (f32[80,24,128]{2,0,1:T(8,128)S(1)}, f32[80,24,128]{2,0,1:T(8,128)}, u32[]{:S(2)}) copy-start(f32[80,24,128]{2,0,1:T(8,128)} %copy-done.6) | copy-start | bytes 2949124
  315.6 42.1 %copy-start.19 = (f32[128]{0:T(128)S(1)}, f32[128]{0:T(128)}, u32[]{:S(2)}) copy-start(f32[128]{0:T(128)} %get-tuple-element.54) | copy-start | bytes 1540
  315.6 55.1 %copy-start.18 = (f32[128]{0:T(128)S(1)}, f32[128]{0:T(128)}, u32[]{:S(2)}) copy-start(f32[128]{0:T(128)} %get-tuple-element.50) | copy-start | bytes 1540
  315.6 75.7 %copy-start.12 = (f32[4,128]{1,0:T(4,128)S(1)}, f32[4,128]{1,0:T(4,128)}, u32[]{:S(2)}) copy-start(f32[4,128]{1,0:T(4,128)} %param.23) | copy-start | bytes 6148
  315.6 76.0 %copy-start.3 = (f32[80,24,128]{2,0,1:T(8,128)S(1)}, f32[80,24,128]{2,0,1:T(8,128)}, u32[]{:S(2)}) copy-start(f32[80,24,128]{2,0,1:T(8,128)} %copy-done.2) | copy-start | bytes 2949124
  (7 other events, 5.7 us)
